TPU v7x, 32 devices: a whole 2x2x4 slice. The times are simulated.
32 devices in a mesh: sc: 4 (over y, x), rows: 8 (over z, core).
Axes of the slice: x: 2, y: 2, z: 4, core: 2. Of those that a mesh axis runs over, the one named last changes fastest.
Arguments:
- embeddings: bfloat16 [32768, 1024], P(('sc', 'rows')), may hold values from -6 to 6
- labels: int32 [32768, 1], P(('sc', 'rows')), may hold values from 0 to 3; in each aligned block of 1024 rows (0 to 1023, 1024 to 2047, ...) at most 512 rows name the same one
- init_idx: int32 [4, 256], P('sc'), may hold values from 0 to 16383
Outputs:
- assign: bfloat16 [32768, 256], P(('sc', 'rows'))
- centroids: float32 [4, 256, 1024], P('sc')
Inputs may be any that keep to these rules, and one draw needn't show every extreme that they name: `labels`: among the rows of one device (aligned blocks of 1024 rows) no label occurs more than 512 times, and some label occurs exactly 512 times; every label occurs somewhere.
All inputs are finite; a program needn't handle non-finite values.
Results may differ from a plain program's by a relative error of at most 0.0052.
Values may be sent and summed in bfloat16 or wider, within the bound.
A program may use at most 64 MiB of HBM per device.

v0:
```python
import math
import jax
import jax.numpy as jnp
from jax import lax
from jax.sharding import PartitionSpec as P

ITERS = 3
ROUNDS = 3


def carried_in(part, axis, combine, identity):
    place = lax.axis_index(axis)
    gathered = lax.all_gather(part, axis)
    state = jnp.zeros_like(part) + jnp.asarray(identity, part.dtype)

    def one(turn, state):
        return combine(state, lax.dynamic_index_in_dim(gathered, turn, 0, False))

    return lax.fori_loop(0, place, one, state)


def unit_of(rows):
    values = rows.astype(jnp.float32)
    scale = lax.rsqrt(jnp.mean(values * values, axis=1, keepdims=True) + 1e-05) * (
        1.0 / math.sqrt(rows.shape[1])
    )
    return (values * scale).astype(jnp.bfloat16)


def unit_cent(mass):
    return (mass * lax.rsqrt(jnp.sum(mass * mass, axis=1, keepdims=True) + 1e-06)).astype(
        jnp.bfloat16
    )


def on_device(embeddings, labels, init_idx):
    tok = embeddings.shape[0]
    width = embeddings.shape[1]
    groups = lax.axis_size("sc")
    slots = 2 * tok // groups
    label_col = labels[:, 0]
    member = (label_col[:, None] == jnp.arange(groups, dtype=jnp.int32)[None, :]).astype(jnp.int32)
    before_here = jnp.cumsum(member, axis=0) - member
    place = jnp.sum(before_here * member, axis=1)
    counts = jnp.sum(member, axis=0).astype(jnp.float32)
    prefix = carried_in(
        counts, ("sc", "rows"), lambda early, later: early + later, jnp.zeros_like(counts)
    )
    totals = lax.psum(counts, ("sc", "rows"))
    prefix_int = prefix.astype(jnp.int32)
    totals_int = totals.astype(jnp.int32)
    rank = jnp.sum(member * prefix_int[None, :], axis=1) + place
    target = label_col * slots + place
    source = (
        jnp.full((groups * slots,), tok, jnp.int32).at[target].set(jnp.arange(tok, dtype=jnp.int32))
    )
    padded = jnp.concatenate([embeddings, jnp.zeros((1, width), jnp.bfloat16)], axis=0)
    rank_pad = jnp.concatenate([rank, jnp.full((1,), -1, jnp.int32)], axis=0)
    outgoing = padded[source].reshape(groups, slots, width)
    out_rank = rank_pad[source].reshape(groups, slots)
    incoming, in_rank = (
        lax.all_to_all(outgoing, "sc", split_axis=0, concat_axis=0, tiled=True),
        lax.all_to_all(out_rank, "sc", split_axis=0, concat_axis=0, tiled=True),
    )
    incoming = incoming.reshape(groups * slots, width)
    in_rank = in_rank.reshape(groups * slots)
    valid = in_rank >= 0
    members = unit_of(incoming)
    group_here = lax.axis_index("sc")
    count = jnp.sum(jnp.where(jnp.arange(groups, dtype=jnp.int32) == group_here, totals_int, 0))
    wanted = init_idx[0] % count
    picker = (wanted[:, None] == in_rank[None, :]).astype(jnp.bfloat16)
    seeds = jnp.dot(picker, members, preferred_element_type=jnp.float32)
    cent = lax.psum(seeds, "rows").astype(jnp.bfloat16)
    contract_rows = (((0,), (0,)), ((), ()))
    contract_width = (((1,), (1,)), ((), ()))
    for round_index in range(ROUNDS):
        scores = lax.dot_general(members, cent, contract_width, preferred_element_type=jnp.float32)
        plan = jnp.where(valid[:, None], jnp.exp(scores * 10.0), 0.0)
        for step in range(ITERS):
            column = lax.psum(jnp.sum(plan, axis=0), "rows")
            plan = plan / column[None, :]
            row_sum = jnp.sum(plan, axis=1)
            plan = jnp.where(valid[:, None], plan / jnp.where(valid, row_sum, 1.0)[:, None], 0.0)
        plan_b = plan.astype(jnp.bfloat16)
        mass_part = lax.dot_general(
            plan_b, members, contract_rows, preferred_element_type=jnp.float32
        )
        if round_index < ROUNDS - 1:
            mass = lax.psum(mass_part, "rows")
            cent = unit_cent(mass)
        else:
            weight_part = jnp.sum(plan, axis=0)
            mass, weight = lax.psum((mass_part, weight_part), "rows")
            means = mass / weight[:, None]
    plan_out = plan.astype(jnp.bfloat16).reshape(groups, slots, plan.shape[1])
    returned = lax.all_to_all(plan_out, "sc", split_axis=0, concat_axis=0, tiled=True).reshape(
        groups * slots, plan.shape[1]
    )
    assign = returned[target]
    return (assign, means[None])


def solution(mesh):
    return jax.shard_map(
        on_device,
        mesh=mesh,
        in_specs=(P(("sc", "rows"), None), P(("sc", "rows"), None), P("sc", None)),
        out_specs=(P(("sc", "rows"), None), P("sc", None, None)),
        check_vma=False,
    )
```

profile of v0, /device:TPU:0, one launch (start us, length us, event | category | flops | bytes accessed | tf_op | source)
XLA Modules:
  0.0 568.7 jit_solution(1118507430221130394)
XLA Ops:
  8.1 42.0 %all-reduce.2 = (f32[128]{0:T(128)S(1)}, f32[4]{0:T(128)S(1)}) all-reduce(f32[128]{0:T(128)S(1)} %convert_dynamic-update-slice_fusion, f32[4]{0:T(128)S(1)} %convert_element_type.59), channel_id=2, replica_groups=mesh['sc'=4,'rows'=8] {'sc','rows'}, use_global_device_ids=true, to_apply=%add.1 | all-reduce | flops 132 | bytes 1056
  54.0 4.3 scatter_custom_fusion
  58.4 20.6 %gather_fusion = s32[2048]{0:T(1024)} fusion(s32[1025]{0:T(1024)S(1)} %pad_add_fusion, s32[2048]{0:T(1024)S(1)} %fusion.27), kind=kCustom, calls=%fused_computation | custom fusion | bytes 24576 | tf_op jit(solution)/shard_map/gather | solution.py:60
  78.9 4.4 all-to-all-start
  85.1 9.7 %gather_fusion.1 = bf16[2048,1024]{1,0:T(8,128)(2,1)} fusion(bf16[1025,1024]{1,0:T(8,128)(2,1)S(1)} %concatenate.7, s32[2048]{0:T(1024)S(1)} %fusion.27), kind=kCustom, calls=%fused_computation.1 | custom fusion | bytes 8396800 | tf_op jit(solution)/shard_map/gather | solution.py:59
  94.8 5.0 all-to-all-start.1
  101.9 44.5 %all-to-all-done.1 = bf16[4,512,1024]{2,1,0:T(8,128)(2,1)} async-done(((bf16[4,512,1024]{2,1,0:T(8,128)(2,1)}), bf16[4,512,1024]{2,1,0:T(8,128)(2,1)}, u32[]{:S(2)}, u32[]{:S(2)}) %all-to-all-start.1) | async-done | bytes 4194336 | tf_op jit(solution)/shard_map/all_to_all | solution.py:62
  146.5 3.1 multiply_reduce_fusion
  149.6 2.9 fusion
  155.8 57.9 %all-reduce.13 = bf16[256,1024]{1,0:T(8,128)(2,1)S(1)} all-reduce(f32[256,1024]{1,0:T(8,128)S(1)} %fusion.7), channel_id=1, replica_groups=mesh['sc'=4,'rows'=8] {'rows'}, use_global_device_ids=true, to_apply=%region_11.12 | all-reduce | flops 262144 | bytes 1572864 | tf_op jit(solution)/shard_map/psum | solution.py:74
  213.7 3.2 fusion.41
  216.8 15.1 %psum.107 = f32[256]{0:T(256)S(1)} all-reduce(f32[256]{0:T(256)S(1)} %get-tuple-element.52), channel_id=1, replica_groups=mesh['sc'=4,'rows'=8] {'rows'}, use_global_device_ids=true, to_apply=%region_13.14 | all-reduce | flops 256 | bytes 2048 | tf_op jit(solution)/shard_map/psum | solution.py:81
  234.3 13.6 %psum.108 = f32[256]{0:T(256)S(1)} all-reduce(f32[256]{0:T(256)S(1)} %get-tuple-element.48), channel_id=1, replica_groups=mesh['sc'=4,'rows'=8] {'rows'}, use_global_device_ids=true, to_apply=%region_16.17 | all-reduce | flops 256 | bytes 2048 | tf_op jit(solution)/shard_map/psum | solution.py:81
  250.0 13.7 %psum.109 = f32[256]{0:T(256)S(1)} all-reduce(f32[256]{0:T(256)S(1)} %get-tuple-element.46), channel_id=1, replica_groups=mesh['sc'=4,'rows'=8] {'rows'}, use_global_device_ids=true, to_apply=%region_19.20 | all-reduce | flops 256 | bytes 2048 | tf_op jit(solution)/shard_map/psum | solution.py:81
  265.7 4.9 fusion.9
  270.9 56.0 %all-reduce.8.cloned.1.call-done = f32[256,1024]{1,0:T(8,128)} async-done(((f32[256,1024]{1,0:T(8,128)}), f32[256,1024]{1,0:T(8,128)}) %all-reduce.8.cloned.1.call-update) | async-done | bytes 1048592 | tf_op jit(solution)/shard_map/psum | solution.py:90
  328.2 3.6 fusion.42
  331.8 13.6 %psum.111 = f32[256]{0:T(256)S(1)} all-reduce(f32[256]{0:T(256)S(1)} %get-tuple-element.54), channel_id=1, replica_groups=mesh['sc'=4,'rows'=8] {'rows'}, use_global_device_ids=true, to_apply=%region_24.25 | all-reduce | flops 256 | bytes 2048 | tf_op jit(solution)/shard_map/psum | solution.py:81
  347.7 13.6 %psum.112 = f32[256]{0:T(256)S(1)} all-reduce(f32[256]{0:T(256)S(1)} %get-tuple-element.44), channel_id=1, replica_groups=mesh['sc'=4,'rows'=8] {'rows'}, use_global_device_ids=true, to_apply=%region_27.28 | all-reduce | flops 256 | bytes 2048 | tf_op jit(solution)/shard_map/psum | solution.py:81
  363.4 13.7 %psum.113 = f32[256]{0:T(256)S(1)} all-reduce(f32[256]{0:T(256)S(1)} %get-tuple-element.42), channel_id=1, replica_groups=mesh['sc'=4,'rows'=8] {'rows'}, use_global_device_ids=true, to_apply=%region_30.31 | all-reduce | flops 256 | bytes 2048 | tf_op jit(solution)/shard_map/psum | solution.py:81
  379.1 4.9 fusion.10
  384.1 57.0 %all-reduce.10.cloned.1.call-done = f32[256,1024]{1,0:T(8,128)} async-done(((f32[256,1024]{1,0:T(8,128)}), f32[256,1024]{1,0:T(8,128)}) %all-reduce.10.cloned.1.call-update) | async-done | bytes 1048592 | tf_op jit(solution)/shard_map/psum | solution.py:90
  442.5 3.6 fusion.43
  446.1 13.6 %psum.115 = f32[256]{0:T(256)S(1)} all-reduce(f32[256]{0:T(256)S(1)} %get-tuple-element.56), channel_id=1, replica_groups=mesh['sc'=4,'rows'=8] {'rows'}, use_global_device_ids=true, to_apply=%region_35.36 | all-reduce | flops 256 | bytes 2048 | tf_op jit(solution)/shard_map/psum | solution.py:81
  462.1 13.6 %psum.116 = f32[256]{0:T(256)S(1)} all-reduce(f32[256]{0:T(256)S(1)} %get-tuple-element.40), channel_id=1, replica_groups=mesh['sc'=4,'rows'=8] {'rows'}, use_global_device_ids=true, to_apply=%region_38.39 | all-reduce | flops 256 | bytes 2048 | tf_op jit(solution)/shard_map/psum | solution.py:81
  478.0 13.6 %psum.117 = f32[256]{0:T(256)S(1)} all-reduce(f32[256]{0:T(256)S(1)} %get-tuple-element.38), channel_id=1, replica_groups=mesh['sc'=4,'rows'=8] {'rows'}, use_global_device_ids=true, to_apply=%region_41.42 | all-reduce | flops 256 | bytes 2048 | tf_op jit(solution)/shard_map/psum | solution.py:81
  494.2 3.5 fusion.44
  497.7 3.6 all-to-all-start.2
  501.3 13.9 %psum.119 = f32[256]{0:T(256)S(1)} all-reduce(f32[256]{0:T(256)S(1)} %get-tuple-element.50), channel_id=1, replica_groups=mesh['sc'=4,'rows'=8] {'rows'}, use_global_device_ids=true, to_apply=%region_45.46 | all-reduce | flops 256 | bytes 2048 | tf_op jit(solution)/shard_map/psum | solution.py:94
  515.2 39.6 %all-reduce.12.cloned.1.call-done = f32[256,1024]{1,0:T(8,128)} async-done(((f32[256,1024]{1,0:T(8,128)}), f32[256,1024]{1,0:T(8,128)}) %all-reduce.12.cloned.1.call-update) | async-done | bytes 1048592 | tf_op jit(solution)/shard_map/psum | solution.py:94
  554.8 2.3 divide_bitcast_fusion
  557.2 5.0 gather_fusion.2
  (83 shorter events, 33.6 us)
Async XLA Ops:
  78.9 15.9 %all-to-all-start = ((s32[4,1,512]{2,1,0:T(1,128)}), s32[4,1,512]{2,1,0:T(1,128)S(1)}, u32[]{:S(2)}, u32[]{:S(2)}) async-start(s32[4,1,512]{2,1,0:T(1,128)} %bitcast.6), calls=%async_computation | async-start | bytes 16384 | tf_op jit(solution)/shard_map/all_to_all | solution.py:63
  94.8 7.0 %copy-start.8 = (s32[1,256]{1,0:T(1,128)S(1)}, s32[1,256]{1,0:T(1,128)}, u32[]{:S(2)}) copy-start(s32[1,256]{1,0:T(1,128)} %param.7) | copy-start | bytes 3076
  94.8 51.7 %all-to-all-start.1 = ((bf16[4,512,1024]{2,1,0:T(8,128)(2,1)}), bf16[4,512,1024]{2,1,0:T(8,128)(2,1)}, u32[]{:S(2)}, u32[]{:S(2)}) async-start(bf16[4,512,1024]{2,1,0:T(8,128)(2,1)} %bitcast.45), calls=%async_computation.1 | async-start | bytes 8388608 | tf_op jit(solution)/shard_map/all_to_all | solution.py:62
  99.8 227.1 %all-reduce.8.cloned.1.call-start = ((), (), s32[]{:S(2)}) async-start(), calls=%async_computation.3 | async-start | bytes 2097152 | tf_op jit(solution)/shard_map/psum | solution.py:90
  152.5 1.9 copy-start.6
  216.8 15.5 %copy-start.3 = (f32[2048,256]{1,0:T(8,128)}, f32[2048,256]{1,0:T(8,128)S(1)}, u32[]{:S(2)}) copy-start(f32[2048,256]{1,0:T(8,128)S(1)} %get-tuple-element.53) | copy-start | bytes 6291460
  250.0 15.7 %copy-start.4 = (f32[2048,256]{1,0:T(8,128)S(1)}, f32[2048,256]{1,0:T(8,128)}, u32[]{:S(2)}) copy-start(f32[2048,256]{1,0:T(8,128)} %get-tuple-element.47) | copy-start | bytes 6291460
  270.6 170.5 %all-reduce.10.cloned.1.call-start = ((), (), s32[]{:S(2)}) async-start(), calls=%async_computation.4 | async-start | bytes 2097152 | tf_op jit(solution)/shard_map/psum | solution.py:90
  331.8 14.0 %copy-start.1 = (f32[2048,256]{1,0:T(8,128)}, f32[2048,256]{1,0:T(8,128)S(1)}, u32[]{:S(2)}) copy-start(f32[2048,256]{1,0:T(8,128)S(1)} %get-tuple-element.55) | copy-start | bytes 6291460
  363.4 15.7 %copy-start.5 = (f32[2048,256]{1,0:T(8,128)S(1)}, f32[2048,256]{1,0:T(8,128)}, u32[]{:S(2)}) copy-start(f32[2048,256]{1,0:T(8,128)} %get-tuple-element.43) | copy-start | bytes 6291460
  384.1 170.8 %all-reduce.12.cloned.1.call-start = ((), (), s32[]{:S(2)}) async-start(), calls=%async_computation.5 | async-start | bytes 2097152 | tf_op jit(solution)/shard_map/psum | solution.py:94
  446.1 14.0 %copy-start.2 = (f32[2048,256]{1,0:T(8,128)}, f32[2048,256]{1,0:T(8,128)S(1)}, u32[]{:S(2)}) copy-start(f32[2048,256]{1,0:T(8,128)S(1)} %get-tuple-element.57) | copy-start | bytes 6291460
  462.1 14.0 %copy-start = (f32[2048,256]{1,0:T(8,128)}, f32[2048,256]{1,0:T(8,128)S(1)}, u32[]{:S(2)}) copy-start(f32[2048,256]{1,0:T(8,128)S(1)} %get-tuple-element.41) | copy-start | bytes 6291460
  491.6 2.6 copy-start.7
  497.7 59.5 %all-to-all-start.2 = ((bf16[4,512,256]{2,1,0:T(8,128)(2,1)}), bf16[4,512,256]{2,1,0:T(8,128)(2,1)S(1)}, u32[]{:S(2)}, u32[]{:S(2)}) async-start(bf16[4,512,256]{2,1,0:T(8,128)(2,1)} %bitcast.11), calls=%async_computation.2 | async-start | bytes 2097152 | tf_op jit(solution)/shard_map/all_to_all | solution.py:97
Sparse Core Ops, SparseCore 0:
  270.8 56.0 all-reduce.7
  384.2 56.9 all-reduce.9
  497.8 56.9 all-reduce.11
where the time goes:
time: 570 us; the launch traced here: 569 us
  blocking collectives  238 us (42%)
  waiting for transfers between devices  197 us (35%)
  local copies, waits for them, and re-layouts  44.2 us (8%)
  other arithmetic  35.6 us (6%)
  matrix products  25 us (4%)
  between operations  15.5 us (3%)
  starting transfers between devices  13.4 us (2%)
    psum x9, blocking collectives, on_device(): column = lax.psum(jnp.sum(plan, axis=0), 'rows')  124 us
    psum x2, waiting for transfers between devices, on_device(): mass = lax.psum(mass_part, 'rows')  113 us
    psum x1, blocking collectives, on_device(): cent = lax.psum(seeds, 'rows').astype(jnp.bfloat16)  57.9 us
    all_to_all x1, waiting for transfers between devices, on_device(): lax.all_to_all(outgoing, 'sc', split_axis=0, concat_axis=0, tiled=True)  44.5 us
    unnamed x1, blocking collectives  42 us
    psum x1, waiting for transfers between devices, on_device(): mass, weight = lax.psum((mass_part, weight_part), 'rows')  39.6 us
    gather x1, local copies, waits for them, and re-layouts, on_device(): out_rank = rank_pad[source].reshape(groups, slots)  20.6 us
    psum x1, blocking collectives, on_device(): mass, weight = lax.psum((mass_part, weight_part), 'rows')  13.9 us
  transfers between devices with their start and end apart: 6, of which 4 were waited for; matrix products, arithmetic and copies ran while one was open for 3% of the time, Pallas kernels for 0%

commit v1 on v0

--- a/solution.py
+++ b/solution.py
@@ -58,8 +58,26 @@
     rank_pad = jnp.concatenate([rank, jnp.full((1,), -1, jnp.int32)], axis=0)
     outgoing = padded[source].reshape(groups, slots, width)
     out_rank = rank_pad[source].reshape(groups, slots)
+
+    def form_blocks(work_x, link_axis):
+        block_last, all_values = (lax.psum(1, link_axis), lax.axis_index(link_axis))
+        even = work_x.shape[0] // block_last
+        z1 = list(work_x.shape)
+        z1[0] = even
+        b_now = z1[0]
+        z1[0] = b_now * block_last
+        now = jnp.zeros(z1, work_x.dtype)
+        for i in range(block_last):
+            placed = lax.dynamic_slice_in_dim(work_x, (all_values ^ i) * even, even, axis=0)
+            if i:
+                placed = lax.ppermute(
+                    placed, link_axis, list(map(lambda at: (at, at ^ i), range(block_last)))
+                )
+            now = lax.dynamic_update_slice_in_dim(now, placed, (all_values ^ i) * b_now, axis=0)
+        return now
+
     incoming, in_rank = (
-        lax.all_to_all(outgoing, "sc", split_axis=0, concat_axis=0, tiled=True),
+        form_blocks(outgoing, "sc"),
         lax.all_to_all(out_rank, "sc", split_axis=0, concat_axis=0, tiled=True),
     )
     incoming = incoming.reshape(groups * slots, width)

time: 570 us -> 550 us (0.965)
  waiting for transfers between devices: 197 us -> 169 us
  local copies, waits for them, and re-layouts: 44.2 us -> 53.9 us
    all_to_all x1 -> x0, waiting for transfers between devices: 44.5 us -> none  [on_device(): lax.all_to_all(outgoing, 'sc', split_axis=0, concat_axis=0, tiled=True)]
    ppermute x0 -> x3, waiting for transfers between devices: none -> 15.2 us  [form_blocks(): lax.ppermute(placed, link_axis, list(map(lambda at: (at, at ^ i), range(b...]
    dynamic_update_slice x0 -> x3, local copies, waits for them, and re-layouts: none -> 6.88 us  [form_blocks(): lax.dynamic_update_slice_in_dim(now, placed, (all_values ^ i) * b_now, ax...]
    ppermute x0 -> x3, starting transfers between devices: none -> 6.63 us  [form_blocks(): lax.ppermute(placed, link_axis, list(map(lambda at: (at, at ^ i), range(b...]
  transfers between devices with their start and end apart: 6 -> 8, of which waited for: 4 -> 4; matrix products, arithmetic and copies ran while one was open for 3% -> 5% of each run, Pallas kernels for 0% -> 0%
where the time goes in v1:
time: 550 us; the launch traced here: 549 us
  blocking collectives  238 us (43%)
  waiting for transfers between devices  169 us (31%)
  local copies, waits for them, and re-layouts  53.9 us (10%)
  other arithmetic  33.5 us (6%)
  matrix products  25 us (5%)
  between operations  15.6 us (3%)
  starting transfers between devices  13.6 us (2%)
    psum x9, blocking collectives, on_device(): column = lax.psum(jnp.sum(plan, axis=0), 'rows')  126 us
    psum x2, waiting for transfers between devices, on_device(): mass = lax.psum(mass_part, 'rows')  114 us
    psum x1, blocking collectives, on_device(): cent = lax.psum(seeds, 'rows').astype(jnp.bfloat16)  56.3 us
    unnamed x1, blocking collectives  42 us
    psum x1, waiting for transfers between devices, on_device(): mass, weight = lax.psum((mass_part, weight_part), 'rows')  39.6 us
    gather x1, local copies, waits for them, and re-layouts, on_device(): out_rank = rank_pad[source].reshape(groups, slots)  20.6 us
    ppermute x3, waiting for transfers between devices, form_blocks(): lax.ppermute(placed, link_axis, list(map(lambda at: (at, at ^ i), range(b...  15.2 us
    psum x1, blocking collectives, on_device(): mass, weight = lax.psum((mass_part, weight_part), 'rows')  13.9 us
  transfers between devices with their start and end apart: 8, of which 4 were waited for; matrix products, arithmetic and copies ran while one was open for 5% of the time, Pallas kernels for 0%

profile of v1, /device:TPU:0, one launch (start us, length us, event | category | flops | bytes accessed | tf_op | source)
XLA Modules:
  0.0 548.9 jit_solution(11140179678903276871)
XLA Ops:
  8.1 42.0 %all-reduce.2 = (f32[128]{0:T(128)S(1)}, f32[4]{0:T(128)S(1)}) all-reduce(f32[128]{0:T(128)S(1)} %convert_dynamic-update-slice_fusion, f32[4]{0:T(128)S(1)} %convert_element_type.59), channel_id=2, replica_groups=mesh['sc'=4,'rows'=8] {'sc','rows'}, use_global_device_ids=true, to_apply=%add.1 | all-reduce | flops 132 | bytes 1056
  54.0 4.3 scatter_custom_fusion
  60.1 9.7 %gather_fusion.1 = bf16[2048,1024]{1,0:T(8,128)(2,1)} fusion(bf16[1025,1024]{1,0:T(8,128)(2,1)S(1)} %concatenate.7, s32[2048]{0:T(1024)S(1)} %fusion.27), kind=kCustom, calls=%fused_computation.1 | custom fusion | bytes 8396800 | tf_op jit(solution)/shard_map/gather | solution.py:59
  72.4 2.6 collective-permute-start
  76.3 20.6 %gather_fusion = s32[2048]{0:T(1024)} fusion(s32[1025]{0:T(1024)S(1)} %pad_add_fusion, s32[2048]{0:T(1024)S(1)} %fusion.27), kind=kCustom, calls=%fused_computation | custom fusion | bytes 24576 | tf_op jit(solution)/shard_map/gather | solution.py:60
  96.8 3.2 all-to-all-start
  100.1 2.8 collective-permute-start.2
  109.7 15.2 %collective-permute-done.2 = bf16[1,512,1024]{2,1,0:T(8,128)(2,1)} collective-permute-done((bf16[1,512,1024]{2,1,0:T(8,128)(2,1)S(1)}, bf16[1,512,1024]{2,1,0:T(8,128)(2,1)}, u32[]{:S(2)}, u32[]{:S(2)}) %collective-permute-start.2) | collective-permute-done | bytes 1048608 | tf_op jit(solution)/shard_map/ppermute | solution.py:73
  127.2 3.2 multiply_reduce_fusion
  134.7 56.3 %all-reduce.13 = bf16[256,1024]{1,0:T(8,128)(2,1)S(1)} all-reduce(f32[256,1024]{1,0:T(8,128)S(1)} %fusion.7), channel_id=1, replica_groups=mesh['sc'=4,'rows'=8] {'rows'}, use_global_device_ids=true, to_apply=%region_11.12 | all-reduce | flops 262144 | bytes 1572864 | tf_op jit(solution)/shard_map/psum | solution.py:92
  191.0 3.2 fusion.41
  194.2 16.7 %psum.107 = f32[256]{0:T(256)S(1)} all-reduce(f32[256]{0:T(256)S(1)} %get-tuple-element.56), channel_id=1, replica_groups=mesh['sc'=4,'rows'=8] {'rows'}, use_global_device_ids=true, to_apply=%region_13.14 | all-reduce | flops 256 | bytes 2048 | tf_op jit(solution)/shard_map/psum | solution.py:99
  213.2 13.6 %psum.108 = f32[256]{0:T(256)S(1)} all-reduce(f32[256]{0:T(256)S(1)} %get-tuple-element.48), channel_id=1, replica_groups=mesh['sc'=4,'rows'=8] {'rows'}, use_global_device_ids=true, to_apply=%region_16.17 | all-reduce | flops 256 | bytes 2048 | tf_op jit(solution)/shard_map/psum | solution.py:99
  228.9 13.9 %psum.109 = f32[256]{0:T(256)S(1)} all-reduce(f32[256]{0:T(256)S(1)} %get-tuple-element.46), channel_id=1, replica_groups=mesh['sc'=4,'rows'=8] {'rows'}, use_global_device_ids=true, to_apply=%region_19.20 | all-reduce | flops 256 | bytes 2048 | tf_op jit(solution)/shard_map/psum | solution.py:99
  244.8 4.9 fusion.9
  249.8 57.2 %all-reduce.8.cloned.1.call-done = f32[256,1024]{1,0:T(8,128)} async-done(((f32[256,1024]{1,0:T(8,128)}), f32[256,1024]{1,0:T(8,128)}) %all-reduce.8.cloned.1.call-update) | async-done | bytes 1048592 | tf_op jit(solution)/shard_map/psum | solution.py:108
  308.3 3.6 fusion.42
  311.9 13.6 %psum.111 = f32[256]{0:T(256)S(1)} all-reduce(f32[256]{0:T(256)S(1)} %get-tuple-element.58), channel_id=1, replica_groups=mesh['sc'=4,'rows'=8] {'rows'}, use_global_device_ids=true, to_apply=%region_24.25 | all-reduce | flops 256 | bytes 2048 | tf_op jit(solution)/shard_map/psum | solution.py:99
  327.9 13.6 %psum.112 = f32[256]{0:T(256)S(1)} all-reduce(f32[256]{0:T(256)S(1)} %get-tuple-element.44), channel_id=1, replica_groups=mesh['sc'=4,'rows'=8] {'rows'}, use_global_device_ids=true, to_apply=%region_27.28 | all-reduce | flops 256 | bytes 2048 | tf_op jit(solution)/shard_map/psum | solution.py:99
  343.6 13.7 %psum.113 = f32[256]{0:T(256)S(1)} all-reduce(f32[256]{0:T(256)S(1)} %get-tuple-element.42), channel_id=1, replica_groups=mesh['sc'=4,'rows'=8] {'rows'}, use_global_device_ids=true, to_apply=%region_30.31 | all-reduce | flops 256 | bytes 2048 | tf_op jit(solution)/shard_map/psum | solution.py:99
  359.2 4.9 fusion.10
  364.2 57.1 %all-reduce.10.cloned.1.call-done = f32[256,1024]{1,0:T(8,128)} async-done(((f32[256,1024]{1,0:T(8,128)}), f32[256,1024]{1,0:T(8,128)}) %all-reduce.10.cloned.1.call-update) | async-done | bytes 1048592 | tf_op jit(solution)/shard_map/psum | solution.py:108
  422.7 3.6 fusion.43
  426.3 13.6 %psum.115 = f32[256]{0:T(256)S(1)} all-reduce(f32[256]{0:T(256)S(1)} %get-tuple-element.60), channel_id=1, replica_groups=mesh['sc'=4,'rows'=8] {'rows'}, use_global_device_ids=true, to_apply=%region_35.36 | all-reduce | flops 256 | bytes 2048 | tf_op jit(solution)/shard_map/psum | solution.py:99
  442.3 13.6 %psum.116 = f32[256]{0:T(256)S(1)} all-reduce(f32[256]{0:T(256)S(1)} %get-tuple-element.40), channel_id=1, replica_groups=mesh['sc'=4,'rows'=8] {'rows'}, use_global_device_ids=true, to_apply=%region_38.39 | all-reduce | flops 256 | bytes 2048 | tf_op jit(solution)/shard_map/psum | solution.py:99
  458.2 13.6 %psum.117 = f32[256]{0:T(256)S(1)} all-reduce(f32[256]{0:T(256)S(1)} %get-tuple-element.38), channel_id=1, replica_groups=mesh['sc'=4,'rows'=8] {'rows'}, use_global_device_ids=true, to_apply=%region_41.42 | all-reduce | flops 256 | bytes 2048 | tf_op jit(solution)/shard_map/psum | solution.py:99
  474.4 3.5 fusion.44
  477.9 3.6 all-to-all-start.1
  481.5 13.9 %psum.119 = f32[256]{0:T(256)S(1)} all-reduce(f32[256]{0:T(256)S(1)} %get-tuple-element.54), channel_id=1, replica_groups=mesh['sc'=4,'rows'=8] {'rows'}, use_global_device_ids=true, to_apply=%region_45.46 | all-reduce | flops 256 | bytes 2048 | tf_op jit(solution)/shard_map/psum | solution.py:112
  495.4 39.6 %all-reduce.12.cloned.1.call-done = f32[256,1024]{1,0:T(8,128)} async-done(((f32[256,1024]{1,0:T(8,128)}), f32[256,1024]{1,0:T(8,128)}) %all-reduce.12.cloned.1.call-update) | async-done | bytes 1048592 | tf_op jit(solution)/shard_map/psum | solution.py:112
  535.0 2.3 divide_bitcast_fusion
  537.3 5.0 gather_fusion.2
  (98 shorter events, 45.0 us)
Async XLA Ops:
  69.8 2.2 copy-start.3
  72.4 3.8 copy-start
  72.4 32.6 %collective-permute-start = (bf16[1,512,1024]{2,1,0:T(8,128)(2,1)S(1)}, bf16[1,512,1024]{2,1,0:T(8,128)(2,1)}, u32[]{:S(2)}, u32[]{:S(2)}) collective-permute-start(bf16[1,512,1024]{2,1,0:T(8,128)(2,1)S(1)} %get-tuple-element.52), channel_id=1, source_target_pairs={{0,8},{8,0},{16,24},{24,16},{1,9},{9,1},{17,25},{25,17},{2,10},{10... | collective-permute-start | bytes 3145736 | tf_op jit(solution)/shard_map/ppermute | solution.py:73
  75.1 32.3 %collective-permute-start.1 = (bf16[1,512,1024]{2,1,0:T(8,128)(2,1)S(1)}, bf16[1,512,1024]{2,1,0:T(8,128)(2,1)}, u32[]{:S(2)}, u32[]{:S(2)}) collective-permute-start(bf16[1,512,1024]{2,1,0:T(8,128)(2,1)S(1)} %get-tuple-element.51), channel_id=1, source_target_pairs={{0,16},{8,24},{16,0},{24,8},{1,17},{9,25},{17,1},{25,9},{2,18},{10... | collective-permute-start | bytes 3145736 | tf_op jit(solution)/shard_map/ppermute | solution.py:73
  76.2 28.6 %copy-start.11 = (s32[1,256]{1,0:T(1,128)S(1)}, s32[1,256]{1,0:T(1,128)}, u32[]{:S(2)}) copy-start(s32[1,256]{1,0:T(1,128)} %param.7) | copy-start | bytes 3076
  96.8 8.2 %all-to-all-start = ((s32[4,1,512]{2,1,0:T(1,128)}), s32[4,1,512]{2,1,0:T(1,128)S(1)}, u32[]{:S(2)}, u32[]{:S(2)}) async-start(s32[4,1,512]{2,1,0:T(1,128)} %bitcast.6), calls=%async_computation | async-start | bytes 16384 | tf_op jit(solution)/shard_map/all_to_all | solution.py:81
  100.1 206.9 %all-reduce.8.cloned.1.call-start = ((), (), s32[]{:S(2)}) async-start(), calls=%async_computation.2 | async-start | bytes 2097152 | tf_op jit(solution)/shard_map/psum | solution.py:108
  100.1 24.8 %collective-permute-start.2 = (bf16[1,512,1024]{2,1,0:T(8,128)(2,1)S(1)}, bf16[1,512,1024]{2,1,0:T(8,128)(2,1)}, u32[]{:S(2)}, u32[]{:S(2)}) collective-permute-start(bf16[1,512,1024]{2,1,0:T(8,128)(2,1)S(1)} %get-tuple-element.50), channel_id=1, source_target_pairs={{0,24},{8,16},{16,8},{24,0},{1,25},{9,17},{17,9},{25,1},{2,26},{10... | collective-permute-start | bytes 3145736 | tf_op jit(solution)/shard_map/ppermute | solution.py:73
  127.2 3.4 copy-start.1
  131.4 1.9 copy-start.9
  194.1 17.1 %copy-start.6 = (f32[2048,256]{1,0:T(8,128)}, f32[2048,256]{1,0:T(8,128)S(1)}, u32[]{:S(2)}) copy-start(f32[2048,256]{1,0:T(8,128)S(1)} %get-tuple-element.57) | copy-start | bytes 6291460
  228.9 15.8 %copy-start.7 = (f32[2048,256]{1,0:T(8,128)S(1)}, f32[2048,256]{1,0:T(8,128)}, u32[]{:S(2)}) copy-start(f32[2048,256]{1,0:T(8,128)} %get-tuple-element.47) | copy-start | bytes 6291460
  249.7 171.6 %all-reduce.10.cloned.1.call-start = ((), (), s32[]{:S(2)}) async-start(), calls=%async_computation.3 | async-start | bytes 2097152 | tf_op jit(solution)/shard_map/psum | solution.py:108
  311.9 14.0 %copy-start.4 = (f32[2048,256]{1,0:T(8,128)}, f32[2048,256]{1,0:T(8,128)S(1)}, u32[]{:S(2)}) copy-start(f32[2048,256]{1,0:T(8,128)S(1)} %get-tuple-element.59) | copy-start | bytes 6291460
  343.6 15.7 %copy-start.8 = (f32[2048,256]{1,0:T(8,128)S(1)}, f32[2048,256]{1,0:T(8,128)}, u32[]{:S(2)}) copy-start(f32[2048,256]{1,0:T(8,128)} %get-tuple-element.43) | copy-start | bytes 6291460
  364.2 170.8 %all-reduce.12.cloned.1.call-start = ((), (), s32[]{:S(2)}) async-start(), calls=%async_computation.4 | async-start | bytes 2097152 | tf_op jit(solution)/shard_map/psum | solution.py:112
  426.3 14.0 %copy-start.5 = (f32[2048,256]{1,0:T(8,128)}, f32[2048,256]{1,0:T(8,128)S(1)}, u32[]{:S(2)}) copy-start(f32[2048,256]{1,0:T(8,128)S(1)} %get-tuple-element.61) | copy-start | bytes 6291460
  442.3 14.0 %copy-start.2 = (f32[2048,256]{1,0:T(8,128)}, f32[2048,256]{1,0:T(8,128)S(1)}, u32[]{:S(2)}) copy-start(f32[2048,256]{1,0:T(8,128)S(1)} %get-tuple-element.41) | copy-start | bytes 6291460
  471.8 2.6 copy-start.10
  477.9 59.5 %all-to-all-start.1 = ((bf16[4,512,256]{2,1,0:T(8,128)(2,1)}), bf16[4,512,256]{2,1,0:T(8,128)(2,1)S(1)}, u32[]{:S(2)}, u32[]{:S(2)}) async-start(bf16[4,512,256]{2,1,0:T(8,128)(2,1)} %bitcast.11), calls=%async_computation.1 | async-start | bytes 2097152 | tf_op jit(solution)/shard_map/all_to_all | solution.py:115
Sparse Core Ops, SparseCore 0:
  249.8 57.0 all-reduce.7
  364.3 56.9 all-reduce.9
  478.0 56.9 all-reduce.11
